TPU v7x, 32 devices: a whole 2x2x4 slice. The times are simulated.
32 devices in a mesh: ctx: 8 (over z, x), head: 4 (over y, core).
Axes of the slice: x: 2, y: 2, z: 4, core: 2. Of those that a mesh axis runs over, the one named last changes fastest.
Arguments:
- q_nope: bfloat16 [1024, 4096], P('ctx', 'head'), may hold values from -6 to 6
- q_rope: bfloat16 [1024, 2048], P('ctx', 'head'), may hold values from -300 to 300
- latent: bfloat16 [1024, 512], P('ctx'), may hold values from -6 to 6
- k_rope: bfloat16 [1024, 64], P('ctx'), may hold values from -4 to 4
- span_order: int32 [16], replicated, may hold values from 0 to 15, each once
- w_uk: bfloat16 [512, 4096], P(None, 'head'), may hold values from -0.25 to 0.25
- w_uv: bfloat16 [512, 4096], P(None, 'head'), may hold values from -0.25 to 0.25
- w_o: bfloat16 [4096, 7168], P('head', 'ctx'), may hold values from -0.125 to 0.125
Outputs:
- attended: bfloat16 [1024, 7168], P('ctx', 'head')
Inputs may be any that keep to these rules, and one draw needn't show every extreme that they name: `span_order`: a permutation of 0 to 15.
All inputs are finite; a program needn't handle non-finite values.
Results may differ from a plain program's by a relative error of at most 0.014.
Values may be sent and summed in bfloat16 or wider, within the bound.
No kernel may reach another device: no remote copies, remote signals or barrier semaphores. Data moves between devices by JAX's collectives and lax.ppermute only.
A program may use at most 128 MiB of HBM per device.

v0:
```python
import math
import jax
import jax.numpy as jnp
from jax import lax
from jax.sharding import PartitionSpec as P

LAT = 512
ROPE = 64
NOPE = 128
VDIM = 128


def span_place(slot_ids, table):
    match = slot_ids[:, None] == jnp.arange(table.shape[0], dtype=jnp.int32)[None, :]
    return jnp.sum(jnp.where(match, table[None, :], 0), axis=1)


def local(q_nope, q_rope, latent, k_rope, span_order, w_uk, w_uv, w_o):
    rows = q_nope.shape[0]
    half = rows // 2
    heads = w_uk.shape[1] // NOPE
    scale = 1.0 / math.sqrt(NOPE + ROPE)
    local_rows = jnp.arange(rows, dtype=jnp.int32)
    query_slot = lax.axis_index("ctx") * 2 + local_rows // half
    qpos = span_place(query_slot, span_order) * half + local_rows % half
    absorbed = jnp.einsum(
        "thn,lhn->htl",
        q_nope.reshape(rows, heads, NOPE),
        w_uk.reshape(LAT, heads, NOPE),
        preferred_element_type=jnp.float32,
    ).astype(jnp.bfloat16)
    rotary = q_rope.reshape(rows, heads, ROPE)
    lat_piece = lax.all_gather(latent, "ctx", axis=0, tiled=True)
    rope_piece = lax.all_gather(k_rope, "ctx", axis=0, tiled=True)
    count = lat_piece.shape[0]
    key_rows = jnp.arange(count, dtype=jnp.int32)
    kpos = span_place(key_rows // half, span_order) * half + key_rows % half
    running = jnp.full((heads, rows), -1e30, jnp.float32)
    score = jnp.einsum("htl,kl->htk", absorbed, lat_piece, preferred_element_type=jnp.float32)
    score = score + jnp.einsum(
        "thr,kr->htk", rotary, rope_piece, preferred_element_type=jnp.float32
    )
    score = score * scale
    visible = kpos[None, None, :] <= qpos[None, :, None]
    newest = jnp.maximum(running, jnp.max(jnp.where(visible, score, -1e30), axis=-1))
    weight = jnp.where(visible, jnp.exp(score - newest[..., None]), 0.0)
    summed = jnp.sum(weight, axis=-1)
    accum = jnp.einsum(
        "htk,kl->htl", weight.astype(jnp.bfloat16), lat_piece, preferred_element_type=jnp.float32
    )
    running, summed, accum = (newest, summed, accum)
    context = (accum / summed[..., None]).astype(jnp.bfloat16)
    heads_out = jnp.einsum(
        "htl,lhv->thv", context, w_uv.reshape(LAT, heads, VDIM), preferred_element_type=jnp.float32
    ).astype(jnp.bfloat16)
    heads_out = heads_out.reshape(rows, heads * VDIM)
    every_token = jnp.dot(
        lax.all_gather(heads_out, "ctx", axis=0, tiled=True),
        w_o,
        preferred_element_type=jnp.float32,
    ).astype(jnp.bfloat16)
    partial_value = lax.all_to_all(every_token, "ctx", split_axis=0, concat_axis=1, tiled=True)
    return (
        lax.psum_scatter(partial_value, "head", scatter_dimension=1, tiled=True)
        .astype(jnp.float32)
        .astype(jnp.bfloat16)
    )


def solution(mesh):
    placed = (
        P("ctx", "head"),
        P("ctx", "head"),
        P("ctx", None),
        P("ctx", None),
        P(),
        P(None, "head"),
        P(None, "head"),
        P("head", "ctx"),
    )
    return jax.shard_map(
        local, mesh=mesh, in_specs=placed, out_specs=P("ctx", "head"), check_vma=False
    )
```

profile of v0, /device:TPU:0, one launch (start us, length us, event | category | flops | bytes accessed | tf_op | source)
XLA Modules:
  0.0 204.4 jit_solution(16470658505095125386)
XLA Ops:
  6.5 0.0 copy-start
  6.5 0.0 all-gather.3.cloned.1.call-start
  6.5 0.7 all-gather.3.cloned.1.call-update
  7.3 0.0 all-gather.5.cloned.1.call-start
  7.3 1.0 copy.19
  8.3 2.3 %copy.24 = bf16[512,1024]{0,1:T(8,128)(2,1)} copy(bf16[512,1024]{1,0:T(8,128)(2,1)} %param.14) | data formatting | bytes 2097152 | tf_op jit(solution)/shard_map/reshape | solution.py:54
  10.6 28.3 %all_gather.10 = bf16[1024,64]{0,1:T(8,128)(2,1)S(1)} all-gather(bf16[128,64]{0,1:T(8,128)(2,1)} %param.11), channel_id=1, replica_groups=mesh['ctx'=8,'head'=4] {'ctx'}, dimensions={0}, use_global_device_ids=true | all-gather | bytes 147456 | tf_op jit(solution)/shard_map/all_gather | solution.py:34
  39.0 0.7 select_reduce_fusion.2
  39.7 0.7 select_reduce_fusion.1
  40.5 0.1 broadcast_compare_fusion
  40.6 12.1 %all-gather.3.cloned.1.call-done = bf16[1024,512]{1,0:T(8,128)(2,1)} async-done(((bf16[128,512]{1,0:T(8,128)(2,1)}), bf16[1024,512]{1,0:T(8,128)(2,1)}) %all-gather.3.cloned.1.call-update) | async-done | bytes 1048592 | tf_op jit(solution)/shard_map/all_gather | solution.py:33
  52.8 5.1 %fusion.8 = f32[8,128,1024]{2,1,0:T(8,128)} fusion(bf16[1024,512]{1,0:T(8,128)(2,1)} %all-gather.3.cloned.1.call-done, bf16[512,1024]{1,0:T(8,128)(2,1)} %param.13, bf16[128,1024]{1,0:T(8,128)(2,1)} %param.8), kind=kOutput, calls=%fused_computation.13 | convolution fusion | flops 1208483840 | bytes 6553600 | tf_op jit(solution)/shard_map/htl,kl->htk/dot_general | solution.py:39
  57.9 3.3 %select_reduce_fusion = (f32[8,128]{1,0:T(8,128)S(1)}, f32[8,128,1024]{2,1,0:T(8,128)S(1)}) fusion(pred[128,1024]{1,0:T(8,128)(4,1)S(1)} %broadcast_compare_fusion, f32[8,128,1024]{2,1,0:T(8,128)} %fusion.8, bf16[128,8,64]{0,2,1:T(8,128)(2,1)S(1)} %bitcast.53, bf16[1024,64]{0,1:T(8,128)(2,1)S(1)} %all_gather.10), kind=kOutput, calls=%fused_computation.3 | convolution fusion | flops 138411008 | bytes 8785920 | tf_op jit(solution)/shard_map/thr,kr->htk/dot_general | solution.py:40
  61.2 1.9 copy-done.1
  63.1 1.1 fusion.1
  64.3 4.8 %convolution_convert_fusion.2 = bf16[8,128,128]{1,2,0:T(8,128)(2,1)} fusion(bf16[512,8,128]{0,2,1:T(8,128)(2,1)} %bitcast.52, f32[8,128]{1,0:T(8,128)S(1)} %fusion.1, f32[8,128,1024]{2,1,0:T(8,128)} %copy-done.1, f32[8,128]{1,0:T(8,128)S(1)} %broadcast_maximum_fusion, pred[128,1024]{1,0:T(8,128)(4,1)S(1)} %broadcast_compare_fusion, ...), kind=kOutput, calls=%fused_computation.14 | convolution fusion | flops 1212284928 | bytes 6692864 | tf_op jit(solution)/shard_map/htl,lhv->thv/dot_general | solution.py:53
  69.1 0.0 all-gather.5.cloned.1.call-update
  69.1 0.0 reduce-scatter.2.cloned.1.call-start
  69.1 49.2 %all-gather.5.cloned.1.call-done = bf16[1024,1024]{0,1:T(8,128)(2,1)} async-done(((bf16[128,1024]{0,1:T(8,128)(2,1)}), bf16[1024,1024]{0,1:T(8,128)(2,1)}) %all-gather.5.cloned.1.call-update) | async-done | bytes 2097168 | tf_op jit(solution)/shard_map/all_gather | solution.py:58
  118.3 4.0 %convolution_convert_fusion = bf16[1024,896]{1,0:T(8,128)(2,1)S(1)} fusion(bf16[1024,1024]{0,1:T(8,128)(2,1)} %all-gather.5.cloned.1.call-done, bf16[1024,896]{1,0:T(8,128)(2,1)S(1)} %copy-done), kind=kOutput, calls=%fused_computation.11 | convolution fusion | flops 1879965696 | bytes 5767168 | tf_op jit(solution)/shard_map/dot_general | solution.py:57
  122.3 45.3 %all_to_all.19 = bf16[8,128,896]{2,1,0:T(8,128)(2,1)S(1)} all-to-all(bf16[8,128,896]{2,1,0:T(8,128)(2,1)S(1)} %bitcast.51), channel_id=1, replica_groups=mesh['ctx'=8,'head'=4] {'ctx'}, dimensions={0} | all-to-all | bytes 3670016 | tf_op jit(solution)/shard_map/all_to_all | solution.py:62
  167.5 1.5 copy.27
  169.1 0.0 reduce-scatter.2.cloned.1.call-update
  169.1 28.8 %reduce-scatter.2.cloned.1.call-done = bf16[128,1792]{1,0:T(8,128)(2,1)} async-done(((bf16[128,7168]{1,0:T(8,128)(2,1)}), bf16[128,1792]{1,0:T(8,128)(2,1)}) %reduce-scatter.2.cloned.1.call-update) | async-done | bytes 458768 | tf_op jit(solution)/shard_map/reduce_scatter | solution.py:64
  (9 shorter events, 0.0 us)
Async XLA Ops:
  6.5 111.8 %copy-start = (bf16[1024,896]{1,0:T(8,128)(2,1)S(1)}, bf16[1024,896]{1,0:T(8,128)(2,1)}, u32[]{:S(2)}) copy-start(bf16[1024,896]{1,0:T(8,128)(2,1)} %param.15) | copy-start | bytes 5505028
  6.5 46.2 %all-gather.3.cloned.1.call-start = ((), (), s32[]{:S(2)}) async-start(), calls=%async_computation.2 | async-start | bytes 1179648 | tf_op jit(solution)/shard_map/all_gather | solution.py:33
  7.3 111.0 %all-gather.5.cloned.1.call-start = ((), (), s32[]{:S(2)}) async-start(), calls=%async_computation.3 | async-start | bytes 2359296 | tf_op jit(solution)/shard_map/all_gather | solution.py:58
  61.2 1.9 copy-start.1
  61.2 3.0 %copy-start.2 = (bf16[1024,512]{1,0:T(8,128)(2,1)S(1)}, bf16[1024,512]{1,0:T(8,128)(2,1)}, u32[]{:S(2)}) copy-start(bf16[1024,512]{1,0:T(8,128)(2,1)} %all-gather.3.cloned.1.call-done) | copy-start | bytes 3145732
  69.1 128.8 %reduce-scatter.2.cloned.1.call-start = ((), (), s32[]{:S(2)}) async-start(), calls=%async_computation.4 | async-start | bytes 2293760 | tf_op jit(solution)/shard_map/reduce_scatter | solution.py:64
Sparse Core Ops, SparseCore 0:
  9.5 43.2 all-gather.2
  69.2 49.0 all-gather.4
  169.2 28.5 reduce-scatter.1
where the time goes:
time: 205 us; the launch traced here: 204 us
  waiting for transfers between devices  90.8 us (44%)
  blocking collectives  73.6 us (36%)
  matrix products  17.2 us (8%)
  between operations  13.2 us (6%)
  local copies, waits for them, and re-layouts  6.76 us (3%)
  other arithmetic  2.76 us (1%)
    all_gather x1, waiting for transfers between devices, local(): lax.all_gather(heads_out, 'ctx', axis=0, tiled=True)  49.2 us
    all_to_all x1, blocking collectives, local(): lax.all_to_all(every_token, 'ctx', split_axis=0, concat_axis=1, tiled=True)  45.3 us
    reduce_scatter x1, waiting for transfers between devices, local(): lax.psum_scatter(partial_value, 'head', scatter_dimension=1, tiled=True)  28.8 us
    all_gather x1, blocking collectives, local(): rope_piece = lax.all_gather(k_rope, 'ctx', axis=0, tiled=True)  28.3 us
    all_gather x1, waiting for transfers between devices, local(): lat_piece = lax.all_gather(latent, 'ctx', axis=0, tiled=True)  12.1 us
    dot_general x1, matrix products, local(): jnp.einsum('htl,kl->htk', absorbed, lat_piece, preferred_element_type=jnp...  5.13 us
    dot_general x1, matrix products, local(): jnp.einsum('htl,lhv->thv', context, w_uv.reshape(LAT, heads, VDIM), prefe...  4.77 us
  transfers between devices with their start and end apart: 3, of which 3 were waited for; matrix products, arithmetic and copies ran while one was open for 2% of the time, Pallas kernels for 0%

commit v1 on v0

--- a/solution.py
+++ b/solution.py
@@ -59,7 +59,12 @@
         w_o,
         preferred_element_type=jnp.float32,
     ).astype(jnp.bfloat16)
-    partial_value = lax.all_to_all(every_token, "ctx", split_axis=0, concat_axis=1, tiled=True)
+    partial_value = jnp.concatenate(
+        lax.all_to_all(
+            jnp.stack(jnp.split(every_token, lax.axis_size("ctx"), axis=0)), "ctx", 0, 0
+        ),
+        axis=1,
+    )
     return (
         lax.psum_scatter(partial_value, "head", scatter_dimension=1, tiled=True)
         .astype(jnp.float32)

time: 205 us -> 208 us (1.015)
  local copies, waits for them, and re-layouts: 6.76 us -> 10.2 us
    reshape x0 -> x1, local copies, waits for them, and re-layouts: none -> 3.77 us  [local(): jnp.concatenate(lax.all_to_all(jnp.stack(jnp.split(every_token, lax.axis_...]
where the time goes in v1:
time: 208 us
  waiting for transfers between devices  92.6 us (45%)
  blocking collectives  73.6 us (35%)
  matrix products  16.8 us (8%)
  between operations  13.3 us (6%)
  local copies, waits for them, and re-layouts  10.2 us (5%)
    all_gather x1, waiting for transfers between devices, local(): lax.all_gather(heads_out, 'ctx', axis=0, tiled=True)  49.2 us
    all_to_all x1, blocking collectives, local(): lax.all_to_all(jnp.stack(jnp.split(every_token, lax.axis_size('ctx'), axi...  45.5 us
    reduce_scatter x1, waiting for transfers between devices, local(): lax.psum_scatter(partial_value, 'head', scatter_dimension=1, tiled=True)  28.7 us
    all_gather x1, blocking collectives, local(): rope_piece = lax.all_gather(k_rope, 'ctx', axis=0, tiled=True)  28.1 us
    all_gather x1, waiting for transfers between devices, local(): lat_piece = lax.all_gather(latent, 'ctx', axis=0, tiled=True)  14 us
    dot_general x1, matrix products, local(): jnp.einsum('htl,lhv->thv', context, w_uv.reshape(LAT, heads, VDIM), prefe...  4.77 us
    dot_general x1, matrix products, local(): jnp.einsum('htl,kl->htk', absorbed, lat_piece, preferred_element_type=jnp...  4.76 us
  transfers between devices with their start and end apart: 3, of which 3 were waited for; matrix products, arithmetic and copies ran while one was open for 2% of the time, Pallas kernels for 0%

profile of v1, /device:TPU:0, one launch (start us, length us, event | category | flops | bytes accessed | tf_op | source)
XLA Modules:
  0.0 208.0 jit_solution(6260573859067052583)
XLA Ops:
  6.5 0.0 all-gather.3.cloned.1.call-start
  6.6 0.7 all-gather.3.cloned.1.call-update
  7.3 0.0 all-gather.5.cloned.1.call-start
  7.3 1.0 copy.19
  8.4 2.3 %copy.25 = bf16[512,1024]{0,1:T(8,128)(2,1)} copy(bf16[512,1024]{1,0:T(8,128)(2,1)} %param.14) | data formatting | bytes 2097152 | tf_op jit(solution)/shard_map/reshape | solution.py:54
  10.7 28.1 %all_gather.10 = bf16[1024,64]{0,1:T(8,128)(2,1)S(1)} all-gather(bf16[128,64]{0,1:T(8,128)(2,1)S(1)} %copy-done.5), channel_id=1, replica_groups=mesh['ctx'=8,'head'=4] {'ctx'}, dimensions={0}, use_global_device_ids=true | all-gather | bytes 147456 | tf_op jit(solution)/shard_map/all_gather | solution.py:34
  38.8 0.1 select_reduce_fusion.2
  38.9 0.1 select_reduce_fusion.1
  39.0 0.1 broadcast_compare_fusion
  39.1 14.0 %all-gather.3.cloned.1.call-done = bf16[1024,512]{1,0:T(8,128)(2,1)} async-done(((bf16[128,512]{1,0:T(8,128)(2,1)}), bf16[1024,512]{1,0:T(8,128)(2,1)}) %all-gather.3.cloned.1.call-update) | async-done | bytes 1048592 | tf_op jit(solution)/shard_map/all_gather | solution.py:33
  53.2 4.8 %fusion.8 = f32[8,128,1024]{2,1,0:T(8,128)} fusion(bf16[1024,512]{1,0:T(8,128)(2,1)} %all-gather.3.cloned.1.call-done, bf16[512,1024]{1,0:T(8,128)(2,1)S(1)} %copy-done.2, bf16[128,1024]{1,0:T(8,128)(2,1)S(1)} %copy-done.4), kind=kOutput, calls=%fused_computation.13 | convolution fusion | flops 1208483840 | bytes 6553600 | tf_op jit(solution)/shard_map/htl,kl->htk/dot_general | solution.py:39
  57.9 3.3 %select_reduce_fusion = (f32[8,128]{1,0:T(8,128)S(1)}, f32[8,128,1024]{2,1,0:T(8,128)S(1)}) fusion(pred[128,1024]{1,0:T(8,128)(4,1)S(1)} %broadcast_compare_fusion, f32[8,128,1024]{2,1,0:T(8,128)} %fusion.8, bf16[128,8,64]{0,2,1:T(8,128)(2,1)S(1)} %bitcast.82, bf16[1024,64]{0,1:T(8,128)(2,1)S(1)} %all_gather.10), kind=kOutput, calls=%fused_computation.3 | convolution fusion | flops 138411008 | bytes 8785920 | tf_op jit(solution)/shard_map/thr,kr->htk/dot_general | solution.py:40
  61.3 1.1 fusion.1
  62.4 0.8 copy-done.1
  63.2 0.1 copy-done.3
  63.3 4.8 %convolution_convert_fusion.2 = bf16[8,128,128]{1,2,0:T(8,128)(2,1)} fusion(bf16[512,8,128]{0,2,1:T(8,128)(2,1)} %bitcast.81, f32[8,128]{1,0:T(8,128)S(1)} %fusion.1, f32[8,128,1024]{2,1,0:T(8,128)} %copy-done.1, f32[8,128]{1,0:T(8,128)S(1)} %broadcast_maximum_fusion, pred[128,1024]{1,0:T(8,128)(4,1)S(1)} %broadcast_compare_fusion, ...), kind=kOutput, calls=%fused_computation.14 | convolution fusion | flops 1212284928 | bytes 6692864 | tf_op jit(solution)/shard_map/htl,lhv->thv/dot_general | solution.py:53
  68.1 0.0 all-gather.5.cloned.1.call-update
  68.1 0.0 reduce-scatter.2.cloned.1.call-start
  68.1 49.2 %all-gather.5.cloned.1.call-done = bf16[1024,1024]{0,1:T(8,128)(2,1)} async-done(((bf16[128,1024]{0,1:T(8,128)(2,1)}), bf16[1024,1024]{0,1:T(8,128)(2,1)}) %all-gather.5.cloned.1.call-update) | async-done | bytes 2097168 | tf_op jit(solution)/shard_map/all_gather | solution.py:58
  117.3 4.0 %convolution_convert_fusion = bf16[1024,896]{1,0:T(8,128)(2,1)S(1)} fusion(bf16[1024,1024]{0,1:T(8,128)(2,1)} %all-gather.5.cloned.1.call-done, bf16[1024,896]{1,0:T(8,128)(2,1)S(1)} %copy-done), kind=kOutput, calls=%fused_computation.11 | convolution fusion | flops 1879965696 | bytes 5767168 | tf_op jit(solution)/shard_map/dot_general | solution.py:57
  121.6 45.5 %all_to_all.5 = bf16[8,128,896]{2,1,0:T(8,128)(2,1)} all-to-all(bf16[8,128,896]{2,1,0:T(8,128)(2,1)S(1)} %fusion.27), channel_id=1, replica_groups=mesh['ctx'=8,'head'=4] {'ctx'}, dimensions={0} | all-to-all | bytes 3670016 | tf_op jit(solution)/shard_map/all_to_all | solution.py:63
  167.0 3.8 %copy.22 = bf16[128,8,896]{0,2,1:T(8,128)(2,1)} copy(bf16[128,8,896]{2,0,1:T(8,128)(2,1)} %bitcast.80) | data formatting | bytes 3670016 | tf_op jit(solution)/shard_map/reshape | solution.py:62
  170.8 28.7 %reduce-scatter.2.cloned.1.call-done = bf16[128,1792]{0,1:T(8,128)(2,1)} async-done(((bf16[128,7168]{0,1:T(8,128)(2,1)}), bf16[128,1792]{0,1:T(8,128)(2,1)}) %reduce-scatter.2.cloned.1.call-update) | async-done | bytes 458768 | tf_op jit(solution)/shard_map/reduce_scatter | solution.py:69
  199.5 2.0 copy.23
  (26 shorter events, 0.3 us)
Async XLA Ops:
  6.5 110.8 %copy-start = (bf16[1024,896]{1,0:T(8,128)(2,1)S(1)}, bf16[1024,896]{1,0:T(8,128)(2,1)}, u32[]{:S(2)}) copy-start(bf16[1024,896]{1,0:T(8,128)(2,1)} %param.15) | copy-start | bytes 5505028
  6.5 4.1 %copy-start.5 = (bf16[128,64]{0,1:T(8,128)(2,1)S(1)}, bf16[128,64]{0,1:T(8,128)(2,1)}, u32[]{:S(2)}) copy-start(bf16[128,64]{0,1:T(8,128)(2,1)} %param.11) | copy-start | bytes 49156
  6.5 32.2 %copy-start.6 = (s32[16]{0:T(128)S(1)}, s32[16]{0:T(128)}, u32[]{:S(2)}) copy-start(s32[16]{0:T(128)} %param.12) | copy-start | bytes 196
  6.5 46.6 %copy-start.2 = (bf16[512,1024]{1,0:T(8,128)(2,1)S(1)}, bf16[512,1024]{1,0:T(8,128)(2,1)}, u32[]{:S(2)}) copy-start(bf16[512,1024]{1,0:T(8,128)(2,1)} %param.13) | copy-start | bytes 3145732
  6.5 46.6 %copy-start.4 = (bf16[128,1024]{1,0:T(8,128)(2,1)S(1)}, bf16[128,1024]{1,0:T(8,128)(2,1)}, u32[]{:S(2)}) copy-start(bf16[128,1024]{1,0:T(8,128)(2,1)} %param.8) | copy-start | bytes 786436
  6.5 46.6 %all-gather.3.cloned.1.call-start = ((), (), s32[]{:S(2)}) async-start(), calls=%async_computation.2 | async-start | bytes 1179648 | tf_op jit(solution)/shard_map/all_gather | solution.py:33
  7.3 110.0 %all-gather.5.cloned.1.call-start = ((), (), s32[]{:S(2)}) async-start(), calls=%async_computation.3 | async-start | bytes 2359296 | tf_op jit(solution)/shard_map/all_gather | solution.py:58
  61.3 1.9 copy-start.1
  61.3 2.0 copy-start.3
  68.1 131.4 %reduce-scatter.2.cloned.1.call-start = ((), (), s32[]{:S(2)}) async-start(), calls=%async_computation.4 | async-start | bytes 2293760 | tf_op jit(solution)/shard_map/reduce_scatter | solution.py:69
Sparse Core Ops, SparseCore 0:
  9.5 43.6 all-gather.2
  68.2 49.0 all-gather.4
  170.9 28.4 reduce-scatter.1
